TPU v7x, 512 devices: a whole 4x8x8 slice. The times are simulated.
512 devices in a mesh: seq: 128 (over y, z, core), mp: 4 (over x).
Axes of the slice: x: 4, y: 8, z: 8, core: 2. Of those that a mesh axis runs over, the one named last changes fastest.
Arguments:
- fresh_queries: bfloat16 [8192, 2048], P('seq', 'mp'), may hold values from -120 to 120
- fresh_keys: bfloat16 [8192, 1024], P('seq', 'mp'), may hold values from -6 to 6
- fresh_values: bfloat16 [8192, 1024], P('seq', 'mp'), may hold values from -6 to 6
- cache: bfloat16 [2, 8192, 1024], P(None, 'seq', 'mp'), may hold values from -6 to 6
- pool_root: int32 [128, 32], replicated, may hold values from 0 to 31
- branch_owner: int32 [128], replicated, may hold values from 0 to 127, each once
- branch_len: int32 [128], replicated, may hold values from 1 to 32, 2048 in all
- branch_root: int32 [128], replicated, may hold values from 0 to 31
- request_branch: int32 [128, 4], P('seq'), may hold values from 0 to 127
- token_request: int32 [128, 64], P('seq'), may hold values from 0 to 3, never falling along the last dimension, each value on 1 to 32 neighbouring positions
- residual: bfloat16 [8192, 2048], P('seq'), may hold values from -1.5 to 1.5
- wo_t: bfloat16 [2048, 2048], P('seq', 'mp'), may hold values from -0.125 to 0.125
- norm_gain: float32 [2048], replicated, may hold values from 0.1 to 1.9
- w_qkv: bfloat16 [2048, 4096], P('seq', 'mp'), may hold values from -0.125 to 0.125
Outputs:
- attn: bfloat16 [8192, 2048], P('seq', 'mp')
- stream: bfloat16 [8192, 2048], P('seq')
- qkv_next: bfloat16 [8192, 4096], P('seq', 'mp')
Inputs may be any that keep to these rules, and one draw needn't show every extreme that they name: `token_request`: in each index's row the request number never falls, and each request has 1 to 32 tokens. `branch_owner`: each index of seq holds exactly one branch. `branch_len`: the longest branch has 32 rows.
All inputs are finite; a program needn't handle non-finite values.
Results may differ from a plain program's by a relative error of at most 0.018.
Values may be sent and summed in bfloat16 or wider, within the bound.
A program may use at most 64 MiB of HBM per device.

v0:
```python
import jax
import jax.numpy as jnp
from jax import lax
from jax.sharding import PartitionSpec as P

QUERY_HEADS = 16
KEY_VALUE_HEADS = 8
HEAD_SIZE = 128


def cache_tags(pool_root, branch_owner, branch_len, root_count, slot_count):
    owner_count = pool_root.shape[0]
    branch_count = branch_owner.shape[0]
    branch_ids = jnp.arange(branch_count, dtype=jnp.int32)
    owner_ids = jnp.arange(owner_count, dtype=jnp.int32)
    owned = jnp.sum(
        jnp.where(branch_owner[None, :] == owner_ids[:, None], branch_ids[None, :], 0), axis=1
    )
    owned_length = jnp.sum(
        jnp.where(branch_ids[None, :] == owned[:, None], branch_len[None, :], 0), axis=1
    )
    slot_ids = jnp.arange(slot_count, dtype=jnp.int32)
    branch_tags = jnp.where(
        slot_ids[None, :] < owned_length[:, None], root_count + owned[:, None], -1
    )
    return jnp.concatenate([pool_root, branch_tags], axis=1).reshape(-1)


def absorb(running, query_rows, key_row_block, value_rows, visible, score_scale):
    peak_old, total, mixed = running
    scores = (
        jnp.einsum("tkgd,rkd->tkgr", query_rows, key_row_block, preferred_element_type=jnp.float32)
        * score_scale
    )
    seen = visible[:, None, None, :]
    peak_new = jnp.maximum(peak_old, jnp.max(jnp.where(seen, scores, -jnp.inf), axis=-1))
    factor = jnp.exp(peak_old - peak_new)
    weights_full = jnp.where(seen, jnp.exp(scores - peak_new[..., None]), 0.0)
    total = total * factor + jnp.sum(weights_full, axis=-1)
    mixed = mixed * factor[..., None] + jnp.einsum(
        "tkgr,rkd->tkgd",
        weights_full.astype(jnp.bfloat16),
        value_rows,
        preferred_element_type=jnp.float32,
    )
    return (peak_new, total, mixed)


def on_device(
    fresh_queries,
    fresh_keys,
    fresh_values,
    cache,
    pool_root,
    branch_owner,
    branch_len,
    branch_root,
    request_branch,
    token_request,
    residual,
    wo_t,
    norm_gain,
    w_qkv,
):
    seq_count = lax.axis_size("seq")
    root_count = seq_count // 4
    tok_rows = fresh_queries.shape[0]
    kv_local = fresh_keys.shape[1] // HEAD_SIZE
    query_groups = QUERY_HEADS // KEY_VALUE_HEADS
    score_scale = HEAD_SIZE ** (-0.5)
    slot_count = cache.shape[1] - pool_root.shape[1]
    tags = cache_tags(pool_root, branch_owner, branch_len, root_count, slot_count)
    requests = token_request[0]
    local_branches = request_branch[0]
    request_ids = jnp.arange(local_branches.shape[0], dtype=jnp.int32)
    token_branch = jnp.sum(
        jnp.where(requests[:, None] == request_ids[None, :], local_branches[None, :], 0), axis=1
    )
    branch_ids = jnp.arange(branch_root.shape[0], dtype=jnp.int32)
    token_root = jnp.sum(
        jnp.where(token_branch[:, None] == branch_ids[None, :], branch_root[None, :], 0), axis=1
    )
    query_rows = fresh_queries.reshape(tok_rows, kv_local, query_groups, HEAD_SIZE)
    incoming_keys = fresh_keys.reshape(tok_rows, kv_local, HEAD_SIZE)
    incoming_values = fresh_values.reshape(tok_rows, kv_local, HEAD_SIZE)
    positions = jnp.arange(tok_rows, dtype=jnp.int32)
    own_visible = (requests[None, :] == requests[:, None]) & (
        positions[None, :] <= positions[:, None]
    )
    start_state = (
        jnp.full((tok_rows, kv_local, query_groups), -jnp.inf, jnp.float32),
        jnp.zeros((tok_rows, kv_local, query_groups), jnp.float32),
        jnp.zeros((tok_rows, kv_local, query_groups, HEAD_SIZE), jnp.float32),
    )
    start_state = absorb(
        start_state, query_rows, incoming_keys, incoming_values, own_visible, score_scale
    )
    state = start_state
    piece = lax.all_gather(cache, "seq", axis=1, tiled=True)
    rows = piece.shape[1]
    block = 512
    key_blocks = piece[0].reshape(rows // block, block, kv_local, HEAD_SIZE)
    value_blocks = piece[1].reshape(rows // block, block, kv_local, HEAD_SIZE)
    tag_blocks = tags.reshape(rows // block, block)

    def one_block(running, parts):
        key_row_block, value_rows, tag_rows = parts
        visible = (tag_rows[None, :] == token_root[:, None]) | (
            tag_rows[None, :] == root_count + token_branch[:, None]
        )
        updated = absorb(running, query_rows, key_row_block, value_rows, visible, score_scale)
        return (updated, None)

    state, unused = lax.scan(one_block, state, (key_blocks, value_blocks, tag_blocks))
    peak_final, total_final, mixed_final = state
    attn = (
        (mixed_final / total_final[..., None])
        .reshape(tok_rows, kv_local * query_groups * HEAD_SIZE)
        .astype(jnp.bfloat16)
    )
    partial_value = lax.dot_general(
        attn,
        lax.all_gather(wo_t, "seq", axis=0, tiled=True),
        (((1,), (1,)), ((), ())),
        preferred_element_type=jnp.float32,
    )
    summed = lax.psum(partial_value.astype(jnp.bfloat16), "mp").astype(jnp.float32)
    stream = (residual.astype(jnp.float32) + summed).astype(jnp.bfloat16)
    widened = stream.astype(jnp.float32)
    mean_square = jnp.mean(widened * widened, axis=-1, keepdims=True)
    normed = (widened * lax.rsqrt(mean_square + 1e-06) * norm_gain[None, :]).astype(jnp.bfloat16)
    qkv_sum = jnp.dot(
        normed, lax.all_gather(w_qkv, "seq", axis=0, tiled=True), preferred_element_type=jnp.float32
    )
    return (attn, stream, qkv_sum.astype(jnp.bfloat16))


def solution(mesh):
    return jax.shard_map(
        on_device,
        mesh=mesh,
        in_specs=(
            P("seq", "mp"),
            P("seq", "mp"),
            P("seq", "mp"),
            P(None, "seq", "mp"),
            P(),
            P(),
            P(),
            P(),
            P("seq", None),
            P("seq", None),
            P("seq", None),
            P("seq", "mp"),
            P(),
            P("seq", "mp"),
        ),
        out_specs=(P("seq", "mp"), P("seq", None), P("seq", "mp")),
        check_vma=False,
    )
```

profile of v0, /device:TPU:1, one launch (start us, length us, event | category | flops | bytes accessed | tf_op | source)
XLA Modules:
  0.0 339.6 jit_solution(17679690994480268077)
XLA Ops:
  7.2 0.7 all-gather.4.cloned.1.call-update
  7.9 0.7 all-gather.6.cloned.1.call-update
  8.7 0.8 fusion.25
  9.5 0.9 reshape.137
  10.4 0.8 reshape.136
  11.4 0.8 reshape.138
  12.2 0.8 select_reduce_fusion.3
  13.0 0.8 select_reduce_fusion.2
  13.8 0.7 pad_add_fusion
  14.7 0.8 select_reduce_fusion.5
  15.7 0.8 select_reduce_fusion.4
  16.6 88.7 %all-gather.4.cloned.1.call-done = bf16[2,8192,256]{2,1,0:T(8,128)(2,1)} async-done(((bf16[2,64,256]{2,1,0:T(8,128)(2,1)}), bf16[2,8192,256]{2,1,0:T(8,128)(2,1)}) %all-gather.4.cloned.1.call-update) | async-done | bytes 8388624 | tf_op jit(solution)/shard_map/all_gather | solution.py:99
  105.3 5.7 %fusion.30 = (bf16[1,8192,256]{2,1,0:T(8,128)(2,1)}, bf16[1,8192,256]{2,1,0:T(8,128)(2,1)}) fusion(bf16[2,8192,256]{2,1,0:T(8,128)(2,1)} %all-gather.4.cloned.1.call-done), kind=kLoop, calls=%fused_computation.64 | loop fusion | bytes 16777216 | tf_op jit(solution)/shard_map/slice | solution.py:103
  111.0 6.9 %reshape.143 = bf16[16,512,2,128]{3,2,1,0:T(2,128)(2,1)} reshape(bf16[1,8192,256]{2,1,0:T(8,128)(2,1)} %get-tuple-element.107) | data formatting | bytes 8388608 | tf_op jit(solution)/shard_map/reshape;squeeze | solution.py:102
  118.0 6.9 %reshape.144 = bf16[16,512,2,128]{3,2,1,0:T(2,128)(2,1)} reshape(bf16[1,8192,256]{2,1,0:T(8,128)(2,1)} %get-tuple-element.106) | data formatting | bytes 8388608 | tf_op jit(solution)/shard_map/reshape;squeeze | solution.py:103
  124.9 39.2 %while.14 = (s32[]{:T(128)}, f32[64,2,2]{0,2,1:T(2,128)S(1)}, f32[64,2,2]{0,2,1:T(2,128)S(1)}, f32[64,2,2,128]{3,0,2,1:T(8,128)S(1)}, s32[16,512]{1,0:T(8,128)S(...) while((s32[]{:T(128)}, f32[64,2,2]{0,2,1:T(2,128)S(1)}, ...), condition=%wide.region_9.10_spmd, body=%wide.region_6.9_spmd.sunk | while | flops 68452928 | bytes 3628149 | solution.py:114
  125.0 1.4 constant_dynamic-slice_fusion.6
  126.4 0.3 select_reduce_fusion.7
  127.0 0.3 fusion.42
  127.5 1.4 constant_dynamic-slice_fusion.6
  128.9 0.3 select_reduce_fusion.7
  129.9 1.4 constant_dynamic-slice_fusion.6
  131.3 0.3 select_reduce_fusion.7
  131.9 0.3 fusion.42
  132.4 1.4 constant_dynamic-slice_fusion.6
  133.8 0.3 select_reduce_fusion.7
  134.4 0.3 fusion.42
  134.8 1.4 constant_dynamic-slice_fusion.6
  136.2 0.3 select_reduce_fusion.7
  137.3 1.4 constant_dynamic-slice_fusion.6
  138.7 0.3 select_reduce_fusion.7
  139.3 0.3 fusion.42
  139.7 1.4 constant_dynamic-slice_fusion.6
  141.1 0.3 select_reduce_fusion.7
  141.7 0.3 fusion.42
  142.2 1.4 constant_dynamic-slice_fusion.6
  143.6 0.3 select_reduce_fusion.7
  144.6 1.4 constant_dynamic-slice_fusion.6
  146.0 0.3 select_reduce_fusion.7
  147.1 1.4 constant_dynamic-slice_fusion.6
  148.5 0.3 select_reduce_fusion.7
  149.1 0.3 fusion.42
  149.5 1.4 constant_dynamic-slice_fusion.6
  150.9 0.3 select_reduce_fusion.7
  152.0 1.4 constant_dynamic-slice_fusion.6
  153.4 0.3 select_reduce_fusion.7
  154.4 1.4 constant_dynamic-slice_fusion.6
  155.8 0.3 select_reduce_fusion.7
  156.4 0.3 fusion.42
  156.9 1.4 constant_dynamic-slice_fusion.6
  158.3 0.3 select_reduce_fusion.7
  159.3 1.4 constant_dynamic-slice_fusion.6
  160.7 0.3 select_reduce_fusion.7
  161.3 0.3 fusion.42
  161.8 1.4 constant_dynamic-slice_fusion.6
  163.2 0.3 select_reduce_fusion.7
  163.8 0.3 fusion.42
  164.3 23.8 %all-gather.6.cloned.1.call-done = bf16[2048,512]{1,0:T(8,128)(2,1)} async-done(((bf16[16,512]{1,0:T(8,128)(2,1)}), bf16[2048,512]{1,0:T(8,128)(2,1)}) %all-gather.6.cloned.1.call-update) | async-done | bytes 2097168 | tf_op jit(solution)/shard_map/all_gather | solution.py:123
  188.1 3.0 convolution_convert_fusion
  191.2 0.5 all-gather.8.cloned.1.call-update
  191.8 46.3 %all-reduce.2.cloned.1.call-done = bf16[64,2048]{1,0:T(8,128)(2,1)} async-done(((bf16[64,2048]{1,0:T(8,128)(2,1)}), bf16[64,2048]{1,0:T(8,128)(2,1)}) %all-reduce.2.cloned.1.call-update) | async-done | bytes 262160 | tf_op jit(solution)/shard_map/psum | solution.py:127
  238.1 1.1 fusion.11
  239.3 90.1 %all-gather.8.cloned.1.call-done = bf16[2048,1024]{1,0:T(8,128)(2,1)} async-done(((bf16[16,1024]{1,0:T(8,128)(2,1)}), bf16[2048,1024]{1,0:T(8,128)(2,1)}) %all-gather.8.cloned.1.call-update) | async-done | bytes 4194320 | tf_op jit(solution)/shard_map/all_gather | solution.py:133
  329.3 3.7 %convolution_convert_fusion.1 = bf16[64,1024]{1,0:T(8,128)(2,1)} fusion(bf16[2048,1024]{1,0:T(8,128)(2,1)} %all-gather.8.cloned.1.call-done, bf16[64,2048]{1,0:T(8,128)(2,1)S(1)} %get-tuple-element.101, f32[2048]{0:T(1024)S(1)} %copy-done.3, f32[64]{0:T(128)S(1)} %add_rsqrt_fusion), kind=kOutput, calls=%fused_computation.22 | convolution fusion | flops 269025280 | bytes 4595968 | tf_op jit(solution)/shard_map/dot_general | solution.py:132
  (145 shorter events, 9.1 us)
Async XLA Ops:
  7.2 98.1 %all-gather.4.cloned.1.call-start = ((), (), s32[]{:S(2)}) async-start(), calls=%async_computation | async-start | bytes 8454144 | tf_op jit(solution)/shard_map/all_gather | solution.py:99
  7.9 180.2 %all-gather.6.cloned.1.call-start = ((), (), s32[]{:S(2)}) async-start(), calls=%async_computation.1 | async-start | bytes 2113536 | tf_op jit(solution)/shard_map/all_gather | solution.py:123
  8.6 229.4 %all-reduce.2.cloned.1.call-start = ((), (), s32[]{:S(2)}) async-start(), calls=%async_computation.2 | async-start | bytes 524288 | tf_op jit(solution)/shard_map/psum | solution.py:127
  124.9 113.2 %copy-start.2 = (bf16[64,2048]{1,0:T(8,128)(2,1)S(1)}, bf16[64,2048]{1,0:T(8,128)(2,1)}, u32[]{:S(2)}) copy-start(bf16[64,2048]{1,0:T(8,128)(2,1)} %param.26) | copy-start | bytes 786436
  124.9 204.4 %copy-start.3 = (f32[2048]{0:T(1024)S(1)}, f32[2048]{0:T(1024)}, u32[]{:S(2)}) copy-start(f32[2048]{0:T(1024)} %param.28) | copy-start | bytes 24580
  164.3 168.7 %copy-start.1 = (bf16[64,512]{1,0:T(8,128)(2,1)}, bf16[64,512]{1,0:T(8,128)(2,1)S(1)}, u32[]{:S(2)}) copy-start(bf16[64,512]{1,0:T(8,128)(2,1)S(1)} %convert_element_type.35) | copy-start | bytes 196612
  191.2 138.1 %all-gather.8.cloned.1.call-start = ((), (), s32[]{:S(2)}) async-start(), calls=%async_computation.3 | async-start | bytes 4227072 | tf_op jit(solution)/shard_map/all_gather | solution.py:133
  239.2 93.8 %copy-start = (bf16[64,2048]{1,0:T(8,128)(2,1)}, bf16[64,2048]{1,0:T(8,128)(2,1)S(1)}, u32[]{:S(2)}) copy-start(bf16[64,2048]{1,0:T(8,128)(2,1)S(1)} %get-tuple-element.101) | copy-start | bytes 786436
Sparse Core Ops, SparseCore 0:
  11.2 94.0 all-gather.3
  108.4 79.6 all-gather.5
  191.3 46.7 all-reduce.1
  241.5 87.7 all-gather.7
where the time goes:
time: 341 us; the launch traced here: 340 us
  waiting for transfers between devices  251 us (74%)
  local copies, waits for them, and re-layouts  44.9 us (13%)
  matrix products  17.1 us (5%)
  between operations  13.9 us (4%)
  other arithmetic  11.8 us (3%)
    all_gather x1, waiting for transfers between devices, on_device(): lax.all_gather(w_qkv, 'seq', axis=0, tiled=True)  90.1 us
    all_gather x1, waiting for transfers between devices, on_device(): piece = lax.all_gather(cache, 'seq', axis=1, tiled=True)  88.7 us
    psum x1, waiting for transfers between devices, on_device(): lax.psum(partial_value.astype(jnp.bfloat16), 'mp').astype(jnp.float32)  46.3 us
    all_gather x1, waiting for transfers between devices, on_device(): lax.all_gather(wo_t, 'seq', axis=0, tiled=True)  23.8 us
    dynamic_slice x32, local copies, waits for them, and re-layouts, on_device(): lax.scan(one_block, state, (key_blocks, value_blocks, tag_blocks))  22.5 us
    another operation x1, local copies, waits for them, and re-layouts, on_device(): value_blocks = piece[1].reshape(rows // block, block, kv_local, HEAD_SIZE)  6.94 us
    another operation x1, local copies, waits for them, and re-layouts, on_device(): key_blocks = piece[0].reshape(rows // block, block, kv_local, HEAD_SIZE)  6.93 us
  transfers between devices with their start and end apart: 4, of which 4 were waited for; matrix products, arithmetic and copies ran while one was open for 20% of the time, Pallas kernels for 0%

commit v1 on v0

--- a/solution.py
+++ b/solution.py
@@ -6,6 +6,11 @@
 QUERY_HEADS = 16
 KEY_VALUE_HEADS = 8
 HEAD_SIZE = 128
+
+
+def exchange_gather(x, mesh_axis, d):
+    sent = jnp.stack([x] * lax.axis_size(mesh_axis))
+    return jnp.concatenate(lax.all_to_all(sent, mesh_axis, 0, 0), axis=d)
 
 
 def cache_tags(pool_root, branch_owner, branch_len, root_count, slot_count):
@@ -120,7 +125,7 @@
     )
     partial_value = lax.dot_general(
         attn,
-        lax.all_gather(wo_t, "seq", axis=0, tiled=True),
+        exchange_gather(wo_t, "seq", 0),
         (((1,), (1,)), ((), ())),
         preferred_element_type=jnp.float32,
     )

time: 341 us -> 346 us (1.015)
  starting transfers between devices: 0.16 us -> 18.5 us
  waiting for transfers between devices: 251 us -> 243 us
  other arithmetic: 11.8 us -> 7.67 us
    all_gather x1 -> x0, waiting for transfers between devices: 23.8 us -> none  [on_device(): lax.all_gather(wo_t, 'seq', axis=0, tiled=True)]
    all_to_all x0 -> x1, starting transfers between devices: none -> 18.4 us  [exchange_gather(): return jnp.concatenate(lax.all_to_all(sent, mesh_axis, 0, 0), axis=d)]
    all_gather x1, waiting for transfers between devices: 88.7 us -> 106 us  [on_device(): piece = lax.all_gather(cache, 'seq', axis=1, tiled=True)]
  transfers between devices with their start and end apart: 4 -> 4, of which waited for: 4 -> 3; matrix products, arithmetic and copies ran while one was open for 20% -> 18% of each run, Pallas kernels for 0% -> 0%
where the time goes in v1:
time: 346 us; the launch traced here: 345 us
  waiting for transfers between devices  243 us (70%)
  local copies, waits for them, and re-layouts  44.8 us (13%)
  starting transfers between devices  18.5 us (5%)
  matrix products  15.5 us (4%)
  between operations  14 us (4%)
  other arithmetic  7.67 us (2%)
    all_gather x1, waiting for transfers between devices, on_device(): piece = lax.all_gather(cache, 'seq', axis=1, tiled=True)  106 us
    all_gather x1, waiting for transfers between devices, on_device(): lax.all_gather(w_qkv, 'seq', axis=0, tiled=True)  90.2 us
    psum x1, waiting for transfers between devices, on_device(): lax.psum(partial_value.astype(jnp.bfloat16), 'mp').astype(jnp.float32)  46 us
    dynamic_slice x32, local copies, waits for them, and re-layouts, on_device(): lax.scan(one_block, state, (key_blocks, value_blocks, tag_blocks))  22.5 us
    all_to_all x1, starting transfers between devices, exchange_gather(): return jnp.concatenate(lax.all_to_all(sent, mesh_axis, 0, 0), axis=d)  18.4 us
    another operation x1, local copies, waits for them, and re-layouts, on_device(): value_blocks = piece[1].reshape(rows // block, block, kv_local, HEAD_SIZE)  6.96 us
  transfers between devices with their start and end apart: 4, of which 3 were waited for; matrix products, arithmetic and copies ran while one was open for 18% of the time, Pallas kernels for 0%

profile of v1, /device:TPU:1, one launch (start us, length us, event | category | flops | bytes accessed | tf_op | source)
XLA Modules:
  0.0 345.1 jit_solution(3544908710710384154)
XLA Ops:
  7.3 0.7 all-gather.3.cloned.1.call-update
  8.0 2.3 stack.2
  10.3 18.4 %all-to-all-start = ((bf16[128,16,512]{2,1,0:T(8,128)(2,1)}), bf16[128,16,512]{2,1,0:T(8,128)(2,1)S(1)}, u32[]{:S(2)}, u32[]{:S(2)}) async-start(bf16[128,16,512]{2,1,0:T(8,128)(2,1)} %stack.2), calls=%async_computation | async-start | bytes 4194304 | tf_op jit(solution)/shard_map/all_to_all | solution.py:13
  30.3 106.0 %all-gather.3.cloned.1.call-done = bf16[2,8192,256]{2,1,0:T(8,128)(2,1)} async-done(((bf16[2,64,256]{2,1,0:T(8,128)(2,1)}), bf16[2,8192,256]{2,1,0:T(8,128)(2,1)}) %all-gather.3.cloned.1.call-update) | async-done | bytes 8388624 | tf_op jit(solution)/shard_map/all_gather | solution.py:104
  136.3 5.7 %fusion.30 = (bf16[1,8192,256]{2,1,0:T(8,128)(2,1)}, bf16[1,8192,256]{2,1,0:T(8,128)(2,1)}) fusion(bf16[2,8192,256]{2,1,0:T(8,128)(2,1)} %all-gather.3.cloned.1.call-done), kind=kLoop, calls=%fused_computation.64 | loop fusion | bytes 16777216 | tf_op jit(solution)/shard_map/slice | solution.py:108
  142.0 6.9 %reshape.150 = bf16[16,512,2,128]{3,2,1,0:T(2,128)(2,1)} reshape(bf16[1,8192,256]{2,1,0:T(8,128)(2,1)} %get-tuple-element.107) | data formatting | bytes 8388608 | tf_op jit(solution)/shard_map/reshape;squeeze | solution.py:107
  148.9 7.0 %reshape.151 = bf16[16,512,2,128]{3,2,1,0:T(2,128)(2,1)} reshape(bf16[1,8192,256]{2,1,0:T(8,128)(2,1)} %get-tuple-element.106) | data formatting | bytes 8388608 | tf_op jit(solution)/shard_map/reshape;squeeze | solution.py:108
  155.8 39.2 %while.14 = (s32[]{:T(128)}, f32[64,2,2]{0,2,1:T(2,128)S(1)}, f32[64,2,2]{0,2,1:T(2,128)S(1)}, f32[64,2,2,128]{3,0,2,1:T(8,128)S(1)}, s32[16,512]{1,0:T(8,128)S(...) while((s32[]{:T(128)}, f32[64,2,2]{0,2,1:T(2,128)S(1)}, ...), condition=%wide.region_9.10_spmd, body=%wide.region_6.9_spmd.sunk | while | flops 68452928 | bytes 3628149 | solution.py:119
  155.9 1.4 constant_dynamic-slice_fusion.6
  157.3 0.3 select_reduce_fusion.7
  157.9 0.3 fusion.42
  158.4 1.4 constant_dynamic-slice_fusion.6
  159.8 0.3 select_reduce_fusion.7
  160.1 0.2 fusion.41
  160.4 0.3 fusion.42
  160.8 1.4 constant_dynamic-slice_fusion.6
  162.2 0.3 select_reduce_fusion.7
  162.8 0.3 fusion.42
  163.3 1.4 constant_dynamic-slice_fusion.6
  164.7 0.3 select_reduce_fusion.7
  165.3 0.3 fusion.42
  165.7 1.4 constant_dynamic-slice_fusion.6
  167.1 0.3 select_reduce_fusion.7
  167.5 0.2 fusion.41
  167.7 0.3 fusion.42
  168.2 1.4 constant_dynamic-slice_fusion.6
  169.6 0.3 select_reduce_fusion.7
  170.2 0.3 fusion.42
  170.6 1.4 constant_dynamic-slice_fusion.6
  172.0 0.3 select_reduce_fusion.7
  172.6 0.3 fusion.42
  173.1 1.4 constant_dynamic-slice_fusion.6
  174.5 0.3 select_reduce_fusion.7
  175.1 0.3 fusion.42
  175.5 1.4 constant_dynamic-slice_fusion.6
  176.9 0.3 select_reduce_fusion.7
  177.5 0.3 fusion.42
  178.0 1.4 constant_dynamic-slice_fusion.6
  179.4 0.3 select_reduce_fusion.7
  180.0 0.3 fusion.42
  180.4 1.4 constant_dynamic-slice_fusion.6
  181.8 0.3 select_reduce_fusion.7
  182.4 0.3 fusion.42
  182.9 1.4 constant_dynamic-slice_fusion.6
  184.3 0.3 select_reduce_fusion.7
  184.9 0.3 fusion.42
  185.3 1.4 constant_dynamic-slice_fusion.6
  186.7 0.3 select_reduce_fusion.7
  187.3 0.3 fusion.42
  187.8 1.4 constant_dynamic-slice_fusion.6
  189.2 0.3 select_reduce_fusion.7
  189.8 0.3 fusion.42
  190.2 1.4 constant_dynamic-slice_fusion.6
  191.6 0.3 select_reduce_fusion.7
  192.2 0.3 fusion.42
  192.7 1.4 constant_dynamic-slice_fusion.6
  194.1 0.3 select_reduce_fusion.7
  194.7 0.3 fusion.42
  195.3 1.5 convolution_convert_fusion
  196.8 0.7 all-gather.5.cloned.1.call-update
  197.5 46.0 %all-reduce.2.cloned.1.call-done = bf16[64,2048]{1,0:T(8,128)(2,1)} async-done(((bf16[64,2048]{1,0:T(8,128)(2,1)}), bf16[64,2048]{1,0:T(8,128)(2,1)}) %all-reduce.2.cloned.1.call-update) | async-done | bytes 262160 | tf_op jit(solution)/shard_map/psum | solution.py:132
  243.5 1.2 fusion.11
  244.6 90.2 %all-gather.5.cloned.1.call-done = bf16[2048,1024]{1,0:T(8,128)(2,1)} async-done(((bf16[16,1024]{1,0:T(8,128)(2,1)}), bf16[2048,1024]{1,0:T(8,128)(2,1)}) %all-gather.5.cloned.1.call-update) | async-done | bytes 4194320 | tf_op jit(solution)/shard_map/all_gather | solution.py:138
  334.8 3.7 %convolution_convert_fusion.1 = bf16[64,1024]{1,0:T(8,128)(2,1)} fusion(bf16[2048,1024]{1,0:T(8,128)(2,1)} %all-gather.5.cloned.1.call-done, bf16[64,2048]{1,0:T(8,128)(2,1)S(1)} %get-tuple-element.101, f32[2048]{0:T(1024)S(1)} %copy-done.7, f32[64]{0:T(128)S(1)} %add_rsqrt_fusion), kind=kOutput, calls=%fused_computation.22 | convolution fusion | flops 269025280 | bytes 4595968 | tf_op jit(solution)/shard_map/dot_general | solution.py:137
  (163 shorter events, 7.2 us)
Async XLA Ops:
  7.2 21.6 %copy-start.3 = (bf16[64,512]{1,0:T(8,128)(2,1)S(1)}, bf16[64,512]{1,0:T(8,128)(2,1)}, u32[]{:S(2)}) copy-start(bf16[64,512]{1,0:T(8,128)(2,1)} %param.16) | copy-start | bytes 196612
  7.2 21.6 %copy-start.4 = (bf16[64,256]{1,0:T(8,128)(2,1)S(1)}, bf16[64,256]{1,0:T(8,128)(2,1)}, u32[]{:S(2)}) copy-start(bf16[64,256]{1,0:T(8,128)(2,1)} %param.17) | copy-start | bytes 98308
  7.2 21.7 %copy-start.5 = (bf16[64,256]{1,0:T(8,128)(2,1)S(1)}, bf16[64,256]{1,0:T(8,128)(2,1)}, u32[]{:S(2)}) copy-start(bf16[64,256]{1,0:T(8,128)(2,1)} %param.18) | copy-start | bytes 98308
  7.2 21.7 %copy-start.9 = (s32[128]{0:T(128)S(1)}, s32[128]{0:T(128)}, u32[]{:S(2)}) copy-start(s32[128]{0:T(128)} %param.21) | copy-start | bytes 1540
  7.2 21.8 %copy-start.10 = (s32[128]{0:T(128)S(1)}, s32[128]{0:T(128)}, u32[]{:S(2)}) copy-start(s32[128]{0:T(128)} %param.22) | copy-start | bytes 1540
  7.2 22.0 %copy-start.6 = (s32[128,32]{0,1:T(8,128)S(1)}, s32[128,32]{0,1:T(8,128)}, u32[]{:S(2)}) copy-start(s32[128,32]{0,1:T(8,128)} %param.20) | copy-start | bytes 49156
  7.2 22.2 %copy-start.8 = (s32[1,64]{1,0:T(1,128)S(1)}, s32[1,64]{1,0:T(1,128)}, u32[]{:S(2)}) copy-start(s32[1,64]{1,0:T(1,128)} %param.25) | copy-start | bytes 772
  7.2 22.2 %copy-start.11 = (s32[1,4]{1,0:T(1,128)S(1)}, s32[1,4]{1,0:T(1,128)}, u32[]{:S(2)}) copy-start(s32[1,4]{1,0:T(1,128)} %param.24) | copy-start | bytes 52
  7.3 22.3 %copy-start.12 = (s32[128]{0:T(128)S(1)}, s32[128]{0:T(128)}, u32[]{:S(2)}) copy-start(s32[128]{0:T(128)} %param.23) | copy-start | bytes 1540
  7.3 129.0 %all-gather.3.cloned.1.call-start = ((), (), s32[]{:S(2)}) async-start(), calls=%async_computation.1 | async-start | bytes 8454144 | tf_op jit(solution)/shard_map/all_gather | solution.py:104
  10.3 184.9 %all-to-all-start = ((bf16[128,16,512]{2,1,0:T(8,128)(2,1)}), bf16[128,16,512]{2,1,0:T(8,128)(2,1)S(1)}, u32[]{:S(2)}, u32[]{:S(2)}) async-start(bf16[128,16,512]{2,1,0:T(8,128)(2,1)} %stack.2), calls=%async_computation | async-start | bytes 4194304 | tf_op jit(solution)/shard_map/all_to_all | solution.py:13
  28.7 214.7 %all-reduce.2.cloned.1.call-start = ((), (), s32[]{:S(2)}) async-start(), calls=%async_computation.2 | async-start | bytes 524288 | tf_op jit(solution)/shard_map/psum | solution.py:132
  155.8 87.7 %copy-start.2 = (bf16[64,2048]{1,0:T(8,128)(2,1)S(1)}, bf16[64,2048]{1,0:T(8,128)(2,1)}, u32[]{:S(2)}) copy-start(bf16[64,2048]{1,0:T(8,128)(2,1)} %param.26) | copy-start | bytes 786436
  155.8 179.0 %copy-start.7 = (f32[2048]{0:T(1024)S(1)}, f32[2048]{0:T(1024)}, u32[]{:S(2)}) copy-start(f32[2048]{0:T(1024)} %param.28) | copy-start | bytes 24580
  195.2 143.3 %copy-start.1 = (bf16[64,512]{1,0:T(8,128)(2,1)}, bf16[64,512]{1,0:T(8,128)(2,1)S(1)}, u32[]{:S(2)}) copy-start(bf16[64,512]{1,0:T(8,128)(2,1)S(1)} %convert_element_type.36) | copy-start | bytes 196612
  196.8 138.1 %all-gather.5.cloned.1.call-start = ((), (), s32[]{:S(2)}) async-start(), calls=%async_computation.3 | async-start | bytes 4227072 | tf_op jit(solution)/shard_map/all_gather | solution.py:138
  244.6 94.0 %copy-start = (bf16[64,2048]{1,0:T(8,128)(2,1)}, bf16[64,2048]{1,0:T(8,128)(2,1)S(1)}, u32[]{:S(2)}) copy-start(bf16[64,2048]{1,0:T(8,128)(2,1)S(1)} %get-tuple-element.101) | copy-start | bytes 786436
Sparse Core Ops, SparseCore 0:
  11.3 124.8 all-gather.2
  196.9 46.5 all-reduce.1
  247.1 87.7 all-gather.4
